TPU v7x, 32 devices: a whole 2x2x4 slice. The times are simulated.
32 devices in a mesh: grp: 4 (over x, core), row: 2 (over y), col: 4 (over z).
Axes of the slice: x: 2, y: 2, z: 4, core: 2. Of those that a mesh axis runs over, the one named last changes fastest.
Arguments:
- density: bfloat16 [256, 15, 128, 128], P(('grp', 'row', 'col')), may hold values from -0.29882812 to 0.29882812
- block_mask: int32 [256, 15], P(('grp', 'row', 'col')), may hold values 0 or 1
- orbital_cell: int32 [32768], P(('grp', 'row', 'col')), may hold values from 0 to 16383
- slab_of_device: int32 [32], replicated, may hold values from 0 to 31, each once
- positions: float32 [3, 16384], P(None, ('grp', 'row', 'col')), may hold values from 0 to 1
- charges: float32 [16384], P(('grp', 'row', 'col')), may hold values from -3 to 3
Outputs:
- new_density: bfloat16 [256, 15, 128, 128], P(('grp', 'row', 'col'))
- energies: float32 [16384], P(('grp', 'row', 'col'))
Inputs may be any that keep to these rules, and one draw needn't show every extreme that they name: `orbital_cell`: cell numbers lie within one slab of 1 planes. `slab_of_device`: a permutation of the slabs.
All inputs are finite; a program needn't handle non-finite values. No bound on the sum of `block_mask` on one device may be relied on, other than what follows from the above.
Results may differ from a plain program's by a relative error of at most 0.0031.
Values may be sent and summed in bfloat16 or wider, within the bound.
No kernel may reach another device: no remote copies, remote signals or barrier semaphores. Data moves between devices by JAX's collectives and lax.ppermute only.
A program may use at most 128 MiB of HBM per device.

v0:
```python
import jax
import jax.numpy as jnp
from jax import lax
from jax.sharding import PartitionSpec as P

BS = 128
BAND = 7
SLOTS = 15
PLANES_DEV = 1
GRID_Y = 128
GRID_Z = 128


SPREAD = 2.0
COUPLE = 0.5
DENSITY_SCALE = 0.05


def with_halo(block, sides, width):
    for axis, dim in sides:
        count = lax.axis_size(axis)
        forward = [(i, i + 1) for i in range(count - 1)]
        backward = [(target, source) for source, target in forward]
        low = lax.ppermute(
            lax.slice_in_dim(block, block.shape[dim] - width, None, axis=dim), axis, forward
        )
        high = lax.ppermute(lax.slice_in_dim(block, 0, width, axis=dim), axis, backward)
        block = jnp.concatenate([low, block, high], axis=dim)
    return block


def gaussian(centre, points):
    offset = points[:, None] - centre[None, :]
    return jnp.exp(-offset * offset / (2.0 * SPREAD * SPREAD))


def atom_tables(positions, grid_x):
    height = jnp.arange(GRID_Y, dtype=jnp.float32)
    depth = jnp.arange(GRID_Z, dtype=jnp.float32)
    return (
        positions[0] * grid_x,
        gaussian(positions[1] * GRID_Y, height),
        gaussian(positions[2] * GRID_Z, depth),
    )


def plane_potential(plane_id, xcoord, along_y, along_z, charges):
    weight = gaussian(xcoord, plane_id.astype(jnp.float32)[None])[0] * charges
    return jnp.dot(along_y * weight[None, :], along_z.T, precision=lax.Precision.HIGHEST)


def plane_energy(rho_plane, plane_id, xcoord, along_y, along_z):
    weight = gaussian(xcoord, plane_id.astype(jnp.float32)[None])[0]
    inner_sum = jnp.dot(rho_plane, along_z, precision=lax.Precision.HIGHEST)
    return weight * jnp.sum(inner_sum * along_y, axis=0)


def make_work(density, valid_blocks, shifts):
    masked = density * valid_blocks.astype(jnp.bfloat16)[:, :, None, None]
    identity = jnp.eye(BS, dtype=jnp.float32)
    centre_block = (
        density[:, BAND].astype(jnp.float32) - shifts[:, :, None] * identity[None]
    ) * valid_blocks[:, BAND][:, None, None]
    return masked.at[:, BAND].set(centre_block.astype(jnp.bfloat16))


def band_square(padded, number):
    results = []
    for slot in range(SLOTS):
        lowest = max(0, slot - BAND)
        highest = min(SLOTS - 1, slot + BAND)
        left_side = padded[BAND : BAND + number, lowest : highest + 1]
        right_side = jnp.stack(
            [
                padded[shift_id : shift_id + number, slot - shift_id + BAND]
                for shift_id in range(lowest, highest + 1)
            ],
            axis=1,
        )
        results.append(
            jnp.einsum("raij,rajk->rik", left_side, right_side, preferred_element_type=jnp.float32)
        )
    return jnp.stack(results, axis=1)


def on_device(density, block_mask, orbital_cell, slab_of_device, positions, charges):
    members = lax.axis_size(("grp", "row", "col"))
    my_index = lax.axis_index(("grp", "row", "col"))
    grid_x = PLANES_DEV * members
    nrows_here = density.shape[0]
    atoms_here = charges.shape[0]
    raw_rows = with_halo(density, ((("grp", "row", "col"), 0),), BAND)
    xcoord, along_y, along_z = atom_tables(positions, grid_x)

    def whole_plane(row_id):
        return slab_of_device[row_id // PLANES_DEV] * PLANES_DEV + row_id % PLANES_DEV

    row_ids = jnp.arange(lax.axis_size(("grp", "row", "col")) * PLANES_DEV, dtype=jnp.int32)
    potential = lax.psum_scatter(
        lax.map(
            lambda row_id: plane_potential(whole_plane(row_id), xcoord, along_y, along_z, charges),
            row_ids,
        ),
        ("grp", "row", "col"),
        scatter_dimension=0,
        tiled=True,
    )
    shifts = (COUPLE * potential.reshape(-1)[orbital_cell]).reshape(nrows_here, BS)
    global_rows = my_index * nrows_here + jnp.arange(nrows_here, dtype=jnp.int32)
    columns = global_rows[:, None] + jnp.arange(SLOTS, dtype=jnp.int32)[None, :] - BAND
    inside = ((columns >= 0) & (columns < nrows_here * members)).astype(jnp.int32)
    valid_blocks = (block_mask * inside).astype(jnp.float32)
    side_table = jnp.concatenate([valid_blocks, shifts], axis=1)
    side_padded = with_halo(side_table, ((("grp", "row", "col"), 0),), BAND)
    padded = make_work(raw_rows, side_padded[:, :SLOTS], side_padded[:, SLOTS:])
    squared = band_square(padded, nrows_here)
    own_rows = padded[BAND : BAND + nrows_here].astype(jnp.float32)
    new_density = (valid_blocks[:, :, None, None] * (2.0 * own_rows - squared)).astype(jnp.bfloat16)
    diagonal_values = (
        jnp.diagonal(new_density[:, BAND], axis1=1, axis2=2).astype(jnp.float32).reshape(-1)
        * DENSITY_SCALE
    )
    cells_here = PLANES_DEV * GRID_Y * GRID_Z
    grid_density = jnp.zeros((cells_here,), jnp.float32).at[orbital_cell].add(diagonal_values)
    grid_density = grid_density.reshape(PLANES_DEV, GRID_Y, GRID_Z)
    piece = lax.all_gather(
        grid_density.astype(jnp.bfloat16), ("grp", "row", "col"), axis=0, tiled=True
    ).astype(jnp.float32)

    def one_row(step_id, accum):
        return accum + plane_energy(piece[step_id], whole_plane(step_id), xcoord, along_y, along_z)

    gathered = lax.fori_loop(0, piece.shape[0], one_row, jnp.zeros((atoms_here,), jnp.float32))
    energies = charges * gathered
    return (new_density, energies)


def solution(mesh):
    in_specs = (
        P(("grp", "row", "col"), None, None, None),
        P(("grp", "row", "col"), None),
        P(("grp", "row", "col")),
        P(),
        P(None, ("grp", "row", "col")),
        P(("grp", "row", "col")),
    )
    out_specs = (P(("grp", "row", "col"), None, None, None), P(("grp", "row", "col")))
    return jax.shard_map(
        on_device, mesh=mesh, in_specs=in_specs, out_specs=out_specs, check_vma=False
    )
```

profile of v0, /device:TPU:0, one launch (start us, length us, event | category | flops | bytes accessed | tf_op | source)
XLA Modules:
  0.0 647.8 jit_solution(2865424066621332306)
XLA Ops:
  8.0 198.7 %while.32 = (s32[]{:T(128)}, f32[32,128,128]{2,1,0:T(8,128)}, s32[32]{0:T(128)S(1)}, s32[32]{0:T(128)}, f32[512]{0:T(512)S(1)}, /*index=5*/f32[512]{0:T(512)}, f...) while((s32[]{:T(128)}, f32[32,128,128]{2,1,0:T(8,128)}, ...), condition=%wide.region_1.2_spmd.clone, body=%wide.region_0.1_spmd.clone.sunk | while | flops 101255688 | bytes 78515 | solution.py:100
  10.6 1.2 dynamic_slice.50
  16.8 1.2 dynamic_slice.50
  23.0 1.2 dynamic_slice.50
  29.2 1.2 dynamic_slice.50
  35.4 1.2 dynamic_slice.50
  41.6 1.2 dynamic_slice.50
  47.9 1.2 dynamic_slice.50
  54.1 1.2 dynamic_slice.50
  60.3 1.2 dynamic_slice.50
  66.5 1.2 dynamic_slice.50
  72.7 1.2 dynamic_slice.50
  78.9 1.2 dynamic_slice.50
  85.1 1.2 dynamic_slice.50
  91.3 1.2 dynamic_slice.50
  97.5 1.2 dynamic_slice.50
  103.7 1.2 dynamic_slice.50
  109.9 1.2 dynamic_slice.50
  116.1 1.2 dynamic_slice.50
  128.6 1.2 dynamic_slice.50
  134.8 1.2 dynamic_slice.50
  159.6 1.2 dynamic_slice.50
  165.8 1.2 dynamic_slice.50
  178.3 1.2 dynamic_slice.50
  203.1 1.2 dynamic_slice.50
  206.9 8.8 %fusion.67 = (bf16[7,15,128,128]{3,2,1,0:T(8,128)(2,1)}, bf16[7,15,128,128]{3,2,1,0:T(8,128)(2,1)}) fusion(bf16[8,15,128,128]{3,2,1,0:T(8,128)(2,1)} %param.12), kind=kLoop, calls=%fused_computation.281 | loop fusion | bytes 13762560 | tf_op jit(solution)/shard_map/slice | solution.py:27
  215.7 6.8 %collective-permute-start = (bf16[7,15,128,128]{3,2,1,0:T(8,128)(2,1)}, bf16[7,15,128,128]{3,2,1,0:T(8,128)(2,1)}, u32[]{:S(2)}, u32[]{:S(2)}) collective-permute-start(bf16[7,15,128,128]{3,2,1,0:T(8,128)(2,1)} %get-tuple-element.577), channel_id=1, source_target_pairs={{0,1},{1,2},{2,3},{3,4},{4,5},{5,6},{6,7},{7,8},{8,9},{9,10},{10,1... | collective-permute-start | bytes 10321928 | tf_op jit(solution)/shard_map/ppermute | solution.py:24
  222.5 1.3 collective-permute-start.1
  225.0 76.2 %collective-permute-done = bf16[7,15,128,128]{3,2,1,0:T(8,128)(2,1)} collective-permute-done((bf16[7,15,128,128]{3,2,1,0:T(8,128)(2,1)}, bf16[7,15,128,128]{3,2,1,0:T(8,128)(2,1)}, u32[]{:S(2)}, u32[]{:S(2)}) %collective-permute-start) | collective-permute-done | bytes 3440672 | tf_op jit(solution)/shard_map/ppermute | solution.py:24
  301.3 4.2 constant_dynamic-update-slice_fusion.2
  305.4 2.2 constant_dynamic-update-slice_fusion.1
  307.6 123.3 %reduce-scatter.2.cloned.1.call-done = f32[1,128,128]{2,1,0:T(8,128)} async-done(((f32[32,128,128]{2,1,0:T(8,128)}), f32[1,128,128]{2,1,0:T(8,128)}) %reduce-scatter.2.cloned.1.call-update) | async-done | bytes 65552 | tf_op jit(solution)/shard_map/reduce_scatter | solution.py:99
  430.9 5.9 gather_fusion
  436.9 2.8 collective-permute-start.2
  439.7 1.3 collective-permute-start.3
  441.0 2.1 constant_dynamic-update-slice_fusion
  443.0 2.2 collective-permute-done.3
  445.5 5.9 broadcast_multiply_fusion
  451.5 1.8 constant_dynamic-update-slice_fusion.172
  454.3 1.5 constant_dynamic-update-slice_fusion.119
  455.8 1.5 constant_dynamic-update-slice_fusion.118
  457.3 1.6 constant_dynamic-update-slice_fusion.133
  458.9 1.3 constant_dynamic-update-slice_fusion.87
  460.2 1.6 constant_dynamic-update-slice_fusion.132
  461.8 1.6 constant_dynamic-update-slice_fusion.131
  467.1 1.4 copy-done.10
  469.3 1.6 constant_dynamic-update-slice_fusion.130
  470.9 1.6 constant_dynamic-update-slice_fusion.129
  472.5 1.6 constant_dynamic-update-slice_fusion.128
  474.1 1.6 constant_dynamic-update-slice_fusion.127
  475.9 1.8 constant_dynamic-update-slice_fusion.125
  477.7 1.4 constant_dynamic-update-slice_fusion.167
  484.5 1.5 copy-done.13
  486.7 2.7 fusion.59
  490.2 2.7 fusion.57
  494.0 3.0 fusion.55
  510.7 2.2 multiply_convert_fusion
  512.9 1.9 copy-done.2
  514.9 3.1 copy.16
  518.1 1.9 gather_fusion.1
  520.1 6.1 scatter_custom_fusion
  526.8 56.6 %all-gather.2.cloned.1.call-done = bf16[32,128,128]{2,1,0:T(8,128)(2,1)} async-done(((bf16[1,128,128]{2,1,0:T(8,128)(2,1)}), bf16[32,128,128]{2,1,0:T(8,128)(2,1)}) %all-gather.2.cloned.1.call-update) | async-done | bytes 1048592 | tf_op jit(solution)/shard_map/all_gather | solution.py:126
  583.5 1.5 convert_element_type.81
  585.0 55.4 %while.33 = (s32[]{:T(128)}, f32[512]{0:T(512)S(1)}, s32[32]{0:T(128)S(1)}, f32[512]{0:T(512)S(1)}, f32[32,128,128]{2,1,0:T(8,128)S(1)}, /*index=5*/f32[512]{0:T(512)S(1)}, f32[512]{0:T(512)S(1)}, s32[]{:T(128)}, s32[]{:T(128)}) while((s32[]{:T(128)}, f32[512]{0:T(512)S(1)}, s32[32]{0:T(128)S(1)}, f32[512]{0:T(512)S(1)}, ...), condition=%wide.region_6.7_spmd.clone, body=%wide.region_4.6_spmd.clone.sunk | while | flops 101321728 | bytes 80003 | solution.py:133
  (315 shorter events, 150.7 us)
Async XLA Ops:
  7.2 423.7 %reduce-scatter.2.cloned.1.call-start = ((), (), s32[]{:S(2)}) async-start(), calls=%async_computation.1 | async-start | bytes 2162688 | tf_op jit(solution)/shard_map/reduce_scatter | solution.py:99
  206.8 8.9 %copy-start.17 = (f32[512]{0:T(512)}, f32[512]{0:T(512)S(1)}, u32[]{:S(2)}) copy-start(f32[512]{0:T(512)S(1)} %get-tuple-element.756) | copy-start | bytes 6148
  206.8 8.9 %copy-start.22 = (f32[512]{0:T(512)}, f32[512]{0:T(512)S(1)}, u32[]{:S(2)}) copy-start(f32[512]{0:T(512)S(1)} %get-tuple-element.764) | copy-start | bytes 6148
  206.8 8.9 %copy-start.24 = (f32[512]{0:T(512)}, f32[512]{0:T(512)S(1)}, u32[]{:S(2)}) copy-start(f32[512]{0:T(512)S(1)} %get-tuple-element.765) | copy-start | bytes 6148
  206.8 17.5 %copy-start.21 = (s32[8,15]{1,0:T(8,128)S(1)}, s32[8,15]{1,0:T(8,128)}, u32[]{:S(2)}) copy-start(s32[8,15]{1,0:T(8,128)} %param.13) | copy-start | bytes 1444
  206.8 17.6 %copy-start.20 = (s32[1024]{0:T(1024)S(1)}, s32[1024]{0:T(1024)}, u32[]{:S(2)}) copy-start(s32[1024]{0:T(1024)} %param.14) | copy-start | bytes 12292
  206.9 376.6 %all-gather.2.cloned.1.call-start = ((), (), s32[]{:S(2)}) async-start(), calls=%async_computation.2 | async-start | bytes 1081344 | tf_op jit(solution)/shard_map/all_gather | solution.py:126
  215.7 85.5 %collective-permute-start = (bf16[7,15,128,128]{3,2,1,0:T(8,128)(2,1)}, bf16[7,15,128,128]{3,2,1,0:T(8,128)(2,1)}, u32[]{:S(2)}, u32[]{:S(2)}) collective-permute-start(bf16[7,15,128,128]{3,2,1,0:T(8,128)(2,1)} %get-tuple-element.577), channel_id=1, source_target_pairs={{0,1},{1,2},{2,3},{3,4},{4,5},{5,6},{6,7},{7,8},{8,9},{9,10},{10,1... | collective-permute-start | bytes 10321928 | tf_op jit(solution)/shard_map/ppermute | solution.py:24
  222.5 218.5 %collective-permute-start.1 = (bf16[7,15,128,128]{3,2,1,0:T(8,128)(2,1)}, bf16[7,15,128,128]{3,2,1,0:T(8,128)(2,1)S(1)}, u32[]{:S(2)}, u32[]{:S(2)}) collective-permute-start(bf16[7,15,128,128]{3,2,1,0:T(8,128)(2,1)} %get-tuple-element.576), channel_id=1, source_target_pairs={{1,0},{2,1},{3,2},{4,3},{5,4},{6,5},{7,6},{8,7},{9,8},{10,9},{11,1... | collective-permute-start | bytes 10321928 | tf_op jit(solution)/shard_map/ppermute | solution.py:27
  225.0 80.4 %copy-start = (bf16[8,15,128,128]{3,2,1,0:T(8,128)(2,1)S(1)}, bf16[8,15,128,128]{3,2,1,0:T(8,128)(2,1)}, u32[]{:S(2)}) copy-start(bf16[8,15,128,128]{3,2,1,0:T(8,128)(2,1)} %param.12) | copy-start | bytes 11796484
  436.9 6.2 collective-permute-start.2
  439.7 5.5 collective-permute-start.3
  467.1 1.4 copy-start.10
  467.1 2.2 copy-start.14
  477.6 5.1 copy-start.3
  477.7 6.3 copy-start.5
  479.0 3.7 copy-start.12
  482.7 1.8 copy-start.6
  482.7 3.3 copy-start.8
  484.5 1.5 copy-start.13
  499.3 2.0 copy-start.4
  501.3 1.9 copy-start.7
  503.2 1.8 copy-start.9
  505.0 1.7 copy-start.11
  506.7 1.7 copy-start.15
  508.4 1.6 copy-start.16
  512.9 1.9 copy-start.2
  514.8 3.2 copy-start.1
  514.9 70.0 %copy-start.18 = (f32[512]{0:T(512)S(1)}, f32[512]{0:T(512)}, u32[]{:S(2)}) copy-start(f32[512]{0:T(512)} %copy-done.17) | copy-start | bytes 6148
  514.9 70.0 %copy-start.23 = (f32[512]{0:T(512)S(1)}, f32[512]{0:T(512)}, u32[]{:S(2)}) copy-start(f32[512]{0:T(512)} %copy-done.22) | copy-start | bytes 6148
  514.9 70.0 %copy-start.25 = (f32[512]{0:T(512)S(1)}, f32[512]{0:T(512)}, u32[]{:S(2)}) copy-start(f32[512]{0:T(512)} %copy-done.24) | copy-start | bytes 6148
  514.9 70.0 %copy-start.26 = (s32[32]{0:T(128)S(1)}, s32[32]{0:T(128)}, u32[]{:S(2)}) copy-start(s32[32]{0:T(128)} %get-tuple-element.766) | copy-start | bytes 388
  526.8 113.6 %copy-start.19 = (f32[512]{0:T(512)S(1)}, f32[512]{0:T(512)}, u32[]{:S(2)}) copy-start(f32[512]{0:T(512)} %get-tuple-element.759) | copy-start | bytes 6148
Sparse Core Ops, SparseCore 0:
  206.9 223.8 reduce-scatter.1
  526.9 56.4 all-gather.1
where the time goes:
time: 651 us; the launch traced here: 648 us
  waiting for transfers between devices  258 us (40%)
  local copies, waits for them, and re-layouts  145 us (22%)
  loops' own time  105 us (16%)
  matrix products  69 us (11%)
  other arithmetic  43.7 us (7%)
  between operations  14.6 us (2%)
  starting transfers between devices  12.2 us (2%)
    reduce_scatter x1, waiting for transfers between devices, on_device(): lax.psum_scatter(lax.map(lambda row_id: plane_potential(whole_plane(row_i...  123 us
    another operation x1, loops' own time, on_device(): lax.map(lambda row_id: plane_potential(whole_plane(row_id), xcoord, along...  83.1 us
    ppermute x2, waiting for transfers between devices, with_halo(): lax.ppermute(lax.slice_in_dim(block, block.shape[dim] - width, None, axis...  76.2 us
    dynamic_slice x64, local copies, waits for them, and re-layouts, whole_plane(): slab_of_device[row_id // PLANES_DEV] * PLANES_DEV + row_id % PLANES_DEV  58.6 us
    all_gather x1, waiting for transfers between devices, on_device(): lax.all_gather(grid_density.astype(jnp.bfloat16), ('grp', 'row', 'col'),...  56.6 us
    unnamed x92, local copies, waits for them, and re-layouts  44.9 us
    dot_general x32, matrix products, plane_potential(): jnp.dot(along_y * weight[None, :], along_z.T, precision=lax.Precision.HIG...  35.1 us
    mul x32, other arithmetic, plane_potential(): weight = gaussian(xcoord, plane_id.astype(jnp.float32)[None])[0] * charges  22.2 us
  transfers between devices with their start and end apart: 6, of which 4 were waited for; matrix products, arithmetic and copies ran while one was open for 4% of the time, Pallas kernels for 0%

commit v1 on v0

v1 whole, which is shorter than its diff:
```python
import functools

import jax
import jax.numpy as jnp
from jax import lax
from jax.experimental import pallas as pl
from jax.experimental.pallas import tpu as pltpu
from jax.sharding import PartitionSpec as P

BS = 128
BAND = 7
SLOTS = 15
PLANES_DEV = 1
GRID_Y = 128
GRID_Z = 128

SPREAD = 2.0
COUPLE = 0.5
DENSITY_SCALE = 0.05

AX = ("grp", "row", "col")
ROWS = 8
EXT = ROWS + 2 * BAND

NEXT_CHUNKS = ((7, 6), (5, 4, 3, 2, 1))
PREV_CHUNKS = ((0, 1), (2, 3, 4, 5, 6))


def next_blocks(rows):
    return [(r, c) for r in rows for c in range(ROWS, r + BAND + 1)]


def prev_blocks(rows):
    return [(r, c) for r in rows for c in range(r - BAND, 0)]


def runs(rows, blocks_of):
    place = 0
    for r in rows:
        blocks = blocks_of((r,))
        yield r, blocks[0][1] - r + BAND, len(blocks), place
        place += len(blocks)


def valid_at(info, mask, r, s):
    row = info[0] * ROWS + r
    column = row + s - BAND
    inside = jnp.logical_and(column >= 0, column < info[1] * ROWS)
    return jnp.where(inside, mask[r, s], 0)


VMEM = pl.BlockSpec(memory_space=pltpu.VMEM)
SMEM = pl.BlockSpec(memory_space=pltpu.SMEM)
ANY = pl.BlockSpec(memory_space=pl.ANY)


def cost(flops, nbytes, exps=0):
    return pl.CostEstimate(flops=int(flops), bytes_accessed=int(nbytes), transcendentals=int(exps))


def pack_kernel(info, mask, density, *refs):
    nchunk = len(NEXT_CHUNKS)
    outs, (scratch, sems) = refs[: 2 * nchunk], refs[2 * nchunk :]
    jobs = []
    for c in range(nchunk):
        for out, rows, blocks_of in (
            (outs[2 * c], PREV_CHUNKS[c], prev_blocks),
            (outs[2 * c + 1], NEXT_CHUNKS[c], next_blocks),
        ):
            for r, s, count, place in runs(rows, blocks_of):
                jobs.append((out, r, s, count, place))
    copies = []
    base = 0
    for j, (out, r, s, count, place) in enumerate(jobs):
        copy = pltpu.make_async_copy(
            density.at[r, pl.ds(s, count)], scratch.at[pl.ds(base, count)], sems.at[j]
        )
        copy.start()
        copies.append((copy, base))
        base += count
    for (out, r, s, count, place), (copy, start) in zip(jobs, copies):
        copy.wait()
        for b in range(count):
            keep = valid_at(info, mask, r, s + b).astype(jnp.float32).astype(jnp.bfloat16)
            out[place + b] = scratch[start + b] * keep


def pack(info, mask, density):
    shapes = []
    for c in range(len(NEXT_CHUNKS)):
        for blocks in (prev_blocks(PREV_CHUNKS[c]), next_blocks(NEXT_CHUNKS[c])):
            shapes.append(jax.ShapeDtypeStruct((len(blocks), BS, BS), jnp.bfloat16))
    total = sum(s.shape[0] for s in shapes)
    return pl.pallas_call(
        pack_kernel,
        out_shape=shapes,
        in_specs=[SMEM, SMEM, ANY],
        out_specs=[VMEM] * len(shapes),
        scratch_shapes=[
            pltpu.VMEM((total, BS, BS), jnp.bfloat16),
            pltpu.SemaphoreType.DMA((2 * BAND,)),
        ],
        cost_estimate=cost(total * BS * BS, 4 * total * BS * BS),
        name="pack",
    )(info, mask, density)


def split(x):
    high = x.astype(jnp.bfloat16)
    return high, (x - high.astype(jnp.float32)).astype(jnp.bfloat16)


def table(centre, points):
    offset = points - centre
    return jnp.exp(offset * offset * (-1.0 / (2.0 * SPREAD * SPREAD)))


def grid_points(lanes):
    return lax.broadcasted_iota(jnp.int32, (GRID_Y, lanes), 0).astype(jnp.float32)


def plane_of(info):
    return (info[2] * PLANES_DEV).astype(jnp.float32)


def shift_kernel(info, atoms, cell, shifts):
    members = atoms.shape[0]
    lanes = atoms.shape[2]
    plane = plane_of(info)
    grid_x = (info[1] * PLANES_DEV).astype(jnp.float32)
    points = grid_points(lanes)

    def step(i, total):
        part = atoms[i]
        weight = table(part[0:1] * grid_x, plane) * part[3:4]
        along_y = table(part[1:2] * GRID_Y, points) * weight
        along_z = table(part[2:3] * GRID_Z, points)
        y_high, y_low = split(along_y)
        z_high, z_low = split(along_z)
        return total + lax.dot_general(
            jnp.concatenate([z_high, z_low], axis=0),
            jnp.concatenate([y_high, y_low], axis=0),
            (((1,), (1,)), ((), ())),
            preferred_element_type=jnp.float32,
        )

    total = lax.fori_loop(0, members, step, jnp.zeros((2 * GRID_Z, 2 * GRID_Y), jnp.float32))
    potential = (
        total[:GRID_Z, :GRID_Y]
        + (total[:GRID_Z, GRID_Y:] + total[GRID_Z:, :GRID_Y])
        + total[GRID_Z:, GRID_Y:]
    )
    high, rest = split(potential)
    middle, low = split(potential - high.astype(jnp.float32))
    cells = cell[...]
    orbitals = cells.shape[1]
    ids = lax.broadcasted_iota(jnp.int32, (GRID_Y, orbitals), 0)
    at_y = (ids == cells // GRID_Z).astype(jnp.float32).astype(jnp.bfloat16)
    stacked = jnp.concatenate([high, middle, low], axis=0)
    picked = jnp.dot(stacked, at_y, preferred_element_type=jnp.float32)
    picked = picked[:GRID_Z] + (picked[GRID_Z : 2 * GRID_Z] + picked[2 * GRID_Z :])
    here = jnp.where(ids == cells % GRID_Z, picked, 0.0)
    shifts[...] = COUPLE * jnp.sum(here, axis=0, keepdims=True)


def shift_values(info, atoms, cell):
    members, _, lanes = atoms.shape
    return pl.pallas_call(
        shift_kernel,
        out_shape=jax.ShapeDtypeStruct(cell.shape, jnp.float32),
        in_specs=[SMEM, VMEM, VMEM],
        out_specs=VMEM,
        cost_estimate=cost(
            2 * 4 * GRID_Y * GRID_Z * members * lanes, 16 * members * lanes, 2 * GRID_Y * members * lanes
        ),
        name="shifts",
    )(info, atoms, cell)


def eye():
    return lax.broadcasted_iota(jnp.int32, (BS, BS), 0) == lax.broadcasted_iota(jnp.int32, (BS, BS), 1)


def work_kernel(info, mask, shifts, density, out):
    diagonal = eye()
    for r in range(ROWS):
        for p in range(EXT):
            s = p - r
            rows, columns = slice(r * BS, (r + 1) * BS), slice(p * BS, (p + 1) * BS)
            if s < 0 or s >= SLOTS:
                out[rows, columns] = jnp.zeros((BS, BS), jnp.bfloat16)
                continue
            keep = valid_at(info, mask, r, s).astype(jnp.float32)
            if s == BAND:
                shift = jnp.where(diagonal, shifts[0:1, rows], 0.0)
                out[rows, columns] = ((density[r, s].astype(jnp.float32) - shift) * keep).astype(jnp.bfloat16)
            else:
                out[rows, columns] = density[r, s] * keep.astype(jnp.bfloat16)


def work_matrix(info, mask, shifts, density):
    return pl.pallas_call(
        work_kernel,
        out_shape=jax.ShapeDtypeStruct((ROWS * BS, EXT * BS), jnp.bfloat16),
        in_specs=[SMEM, SMEM, VMEM, VMEM],
        out_specs=VMEM,
        cost_estimate=cost(ROWS * SLOTS * BS * BS, 4 * ROWS * EXT * BS * BS),
        name="work",
    )(info, mask, shifts, density)


def mine(first, last):
    return slice((first + BAND) * BS, (last + BAND) * BS)


def groups(rows):
    return [rows[i : i + 2] for i in range(0, len(rows), 2)]


def partial_kernel(chunk, work, above, below, to_prev, to_next, strip):
    for packed, out, rows, blocks_of, down in (
        (above, to_prev, NEXT_CHUNKS[chunk], next_blocks, True),
        (below, to_next, PREV_CHUNKS[chunk], prev_blocks, False),
    ):
        places = {r: (count, place) for r, _, count, place in runs(rows, blocks_of)}
        for group in groups(rows):
            width = max(places[r][0] for r in group)
            for g, r in enumerate(group):
                count, place = places[r]
                pad = 0 if down else width - count
                for b in range(width):
                    inside = pad <= b < pad + count
                    strip[g * BS : (g + 1) * BS, b * BS : (b + 1) * BS] = (
                        packed[place + b - pad] if inside else jnp.zeros((BS, BS), jnp.bfloat16)
                    )
            first, last = (0, width) if down else (ROWS - width, ROWS)
            product = jnp.dot(
                strip[: len(group) * BS, : width * BS],
                work[first * BS : last * BS, mine(first, last)],
                preferred_element_type=jnp.float32,
            ).astype(jnp.bfloat16)
            for g, r in enumerate(group):
                count, place = places[r]
                pad = 0 if down else width - count
                for b in range(count):
                    out[place + b] = product[g * BS : (g + 1) * BS, (pad + b) * BS : (pad + b + 1) * BS]


def partial_products(chunk, work, above, below):
    n_next, n_prev = above.shape[0], below.shape[0]
    return pl.pallas_call(
        functools.partial(partial_kernel, chunk),
        out_shape=[
            jax.ShapeDtypeStruct(above.shape, jnp.bfloat16),
            jax.ShapeDtypeStruct(below.shape, jnp.bfloat16),
        ],
        in_specs=[VMEM, VMEM, VMEM],
        out_specs=[VMEM, VMEM],
        scratch_shapes=[pltpu.VMEM((2 * BS, BAND * BS), jnp.bfloat16)],
        cost_estimate=cost(2 * 5 * (n_next + n_prev) * BS**3, 4 * ROWS * EXT * BS * BS),
        name=f"partial{chunk}",
    )(work, above, below)


def own_kernel(info, mask, work, *refs):
    nchunk = len(NEXT_CHUNKS)
    received = refs[: 2 * nchunk]
    out, diagonal_out, right, result, sems = refs[2 * nchunk :]
    size = ROWS * BS
    right[: BAND * BS] = jnp.zeros((BAND * BS, size), jnp.bfloat16)
    right[(BAND + ROWS) * BS :] = jnp.zeros((BAND * BS, size), jnp.bfloat16)
    right[BAND * BS : (BAND + ROWS) * BS] = work[:, mine(0, ROWS)]
    for c in range(nchunk):
        above, below = received[2 * c], received[2 * c + 1]
        for b, (r, column) in enumerate(next_blocks(NEXT_CHUNKS[c])):
            k, j = r - ROWS + BAND, column - ROWS
            right[k * BS : (k + 1) * BS, j * BS : (j + 1) * BS] = above[b]
        for b, (r, column) in enumerate(prev_blocks(PREV_CHUNKS[c])):
            k, j = r + ROWS + BAND, column + ROWS
            right[k * BS : (k + 1) * BS, j * BS : (j + 1) * BS] = below[b]
    on_diagonal = eye()
    copies = []
    for pair in range(ROWS // 2):
        first = 2 * pair
        squared = jnp.dot(
            work[first * BS : (first + 2) * BS, first * BS : (first + 16) * BS],
            right[first * BS : (first + 16) * BS, :],
            preferred_element_type=jnp.float32,
        )
        for g in range(2):
            r = first + g
            for j in range(ROWS):
                keep = valid_at(info, mask, r, j - r + BAND).astype(jnp.float32)
                mine_now = work[r * BS : (r + 1) * BS, mine(j, j + 1)].astype(jnp.float32)
                value = keep * (2.0 * mine_now - squared[g * BS : (g + 1) * BS, j * BS : (j + 1) * BS])
                value = value.astype(jnp.bfloat16)
                result[r, j] = value
                if j == r:
                    kept = jnp.where(on_diagonal, value.astype(jnp.float32), 0.0)
                    diagonal_out[0:1, r * BS : (r + 1) * BS] = jnp.sum(kept, axis=0, keepdims=True)
            copy = pltpu.make_async_copy(result.at[r], out.at[r, pl.ds(BAND - r, ROWS)], sems.at[r])
            copy.start()
            copies.append(copy)
    for copy in copies:
        copy.wait()


def own_products(info, mask, work, received, shape):
    size = ROWS * BS
    return pl.pallas_call(
        own_kernel,
        out_shape=[
            jax.ShapeDtypeStruct(shape, jnp.bfloat16),
            jax.ShapeDtypeStruct((1, size), jnp.float32),
        ],
        in_specs=[SMEM, SMEM, VMEM] + [VMEM] * len(received),
        out_specs=[ANY, VMEM],
        scratch_shapes=[
            pltpu.VMEM((EXT * BS, size), jnp.bfloat16),
            pltpu.VMEM((ROWS, ROWS, BS, BS), jnp.bfloat16),
            pltpu.SemaphoreType.DMA((ROWS,)),
        ],
        cost_estimate=cost(2 * size * size * 2048, 4 * size * EXT * BS),
        name="own",
    )(info, mask, work, *received)


def side_kernel(work, to_next, to_prev):
    nxt = {b: i for i, b in enumerate(next_blocks(range(1, ROWS)))}
    prv = {b: i for i, b in enumerate(prev_blocks(range(ROWS - 1)))}
    for pair in range(ROWS // 2):
        first = 2 * pair
        rows = slice(first * BS, (first + 2) * BS)
        for places, out, lo, hi, k0, k1 in (
            (nxt, to_next, ROWS, first + 1 + BAND + 1, 1, ROWS),
            (prv, to_prev, first - BAND, 0, 0, ROWS - 1),
        ):
            squared = jnp.dot(
                work[rows, mine(k0, k1)],
                work[k0 * BS : k1 * BS, mine(lo, hi)],
                preferred_element_type=jnp.float32,
            )
            for g in range(2):
                r = first + g
                for c in range(lo, hi):
                    if (r, c) not in places:
                        continue
                    own = work[r * BS : (r + 1) * BS, mine(c, c + 1)].astype(jnp.float32)
                    out[places[r, c]] = (
                        2.0 * own - squared[g * BS : (g + 1) * BS, (c - lo) * BS : (c - lo + 1) * BS]
                    )


def side_products(work):
    count = BAND * (BAND + 1) // 2
    shape = jax.ShapeDtypeStruct((count, BS, BS), jnp.float32)
    return pl.pallas_call(
        side_kernel,
        out_shape=[shape, shape],
        in_specs=[VMEM],
        out_specs=[VMEM, VMEM],
        cost_estimate=cost(2 * 9 * count * BS**3, 4 * ROWS * BS * EXT * BS),
        name="side",
    )(work)


def finish_kernel(info, mask, at_next, at_prev, *refs):
    nchunk = len(NEXT_CHUNKS)
    received = refs[: 2 * nchunk]
    _, out, result, sems = refs[2 * nchunk :]
    nxt = {b: i for i, b in enumerate(next_blocks(range(1, ROWS)))}
    prv = {b: i for i, b in enumerate(prev_blocks(range(ROWS - 1)))}
    copies = []
    base = 0
    for c in range(nchunk):
        for packed, local, places, rows, blocks_of in (
            (received[2 * c], at_next, nxt, NEXT_CHUNKS[c], next_blocks),
            (received[2 * c + 1], at_prev, prv, PREV_CHUNKS[c], prev_blocks),
        ):
            for r, s, count, place in runs(rows, blocks_of):
                for b in range(count):
                    keep = valid_at(info, mask, r, s + b).astype(jnp.float32)
                    value = local[places[r, s + b + r - BAND]] - packed[place + b].astype(jnp.float32)
                    result[base + b] = (keep * value).astype(jnp.bfloat16)
                copy = pltpu.make_async_copy(
                    result.at[pl.ds(base, count)], out.at[r, pl.ds(s, count)], sems.at[len(copies)]
                )
                copy.start()
                copies.append(copy)
                base += count
    for copy in copies:
        copy.wait()


def finish(info, mask, at_next, at_prev, received, new_density):
    count = BAND * (BAND + 1)
    operands = [info, mask, at_next, at_prev, *received, new_density]
    return pl.pallas_call(
        finish_kernel,
        out_shape=jax.ShapeDtypeStruct(new_density.shape, new_density.dtype),
        in_specs=[SMEM, SMEM] + [VMEM] * (2 + len(received)) + [ANY],
        out_specs=ANY,
        scratch_shapes=[
            pltpu.VMEM((count, BS, BS), jnp.bfloat16),
            pltpu.SemaphoreType.DMA((2 * BAND,)),
        ],
        input_output_aliases={len(operands) - 1: 0},
        cost_estimate=cost(3 * count * BS * BS, 8 * count * BS * BS),
        name="finish",
    )(*operands)


def energy_kernel(info, atoms, cell, diagonal, out):
    members = atoms.shape[0]
    lanes = atoms.shape[2]
    plane = plane_of(info)
    grid_x = (info[1] * PLANES_DEV).astype(jnp.float32)
    points = grid_points(lanes)
    cells = cell[...]
    ids = lax.broadcasted_iota(jnp.int32, (GRID_Y, cells.shape[1]), 0)
    at_y = jnp.where(ids == cells // GRID_Z, diagonal[...], 0.0).astype(jnp.bfloat16)
    at_z = (ids == cells % GRID_Z).astype(jnp.float32).astype(jnp.bfloat16)
    rho = lax.dot_general(
        at_y, at_z, (((1,), (1,)), ((), ())), preferred_element_type=jnp.float32
    )
    high, low = split(rho * DENSITY_SCALE)
    rho_wide = jnp.concatenate([high, high], axis=1)

    def step(i, carry):
        part = atoms[i]
        weight = table(part[0:1] * grid_x, plane)
        along_y = table(part[1:2] * GRID_Y, points)
        z_high, z_low = split(table(part[2:3] * GRID_Z, points))
        inner = jnp.dot(
            rho_wide, jnp.concatenate([z_high, z_low], axis=0), preferred_element_type=jnp.float32
        ) + jnp.dot(low, z_high, preferred_element_type=jnp.float32)
        energy = jnp.sum(inner * along_y, axis=0, keepdims=True) * weight
        for q in range(lanes // BS):
            out[i, q : q + 1, :] = energy[:, q * BS : (q + 1) * BS]
        return carry

    lax.fori_loop(0, members, step, 0)


def energy_shares(info, atoms, cell, diagonal):
    members, _, lanes = atoms.shape
    return pl.pallas_call(
        energy_kernel,
        out_shape=jax.ShapeDtypeStruct((members, lanes // BS, BS), jnp.float32),
        in_specs=[SMEM, VMEM, VMEM, VMEM],
        out_specs=VMEM,
        cost_estimate=cost(
            2 * 3 * GRID_Y * GRID_Z * members * lanes, 16 * members * lanes, 2 * GRID_Y * members * lanes
        ),
        name="energy",
    )(info, atoms, cell, diagonal)


def on_device(density, block_mask, orbital_cell, slab_of_device, positions, charges):
    members = lax.axis_size(AX)
    my_index = lax.axis_index(AX)
    info = jnp.stack([my_index, jnp.int32(members), slab_of_device[my_index]]).astype(jnp.int32)
    forward = [(i, i + 1) for i in range(members - 1)]
    backward = [(i + 1, i) for i in range(members - 1)]
    chunks = range(len(NEXT_CHUNKS))

    packed = pack(info, block_mask, density)
    above = [lax.ppermute(packed[2 * c + 1], AX, forward) for c in chunks]
    below = [lax.ppermute(packed[2 * c], AX, backward) for c in chunks]

    atoms = jnp.concatenate([positions, charges[None]], axis=0)[None]
    for axis in reversed(AX):
        atoms = lax.all_gather(atoms, axis, axis=0, tiled=True)
    cell = orbital_cell[None]
    shifts = shift_values(info, atoms, cell)
    work = work_matrix(info, block_mask, shifts, density)

    back_next, back_prev, received = [], [], []
    for c in chunks:
        to_prev, to_next = partial_products(c, work, above[c], below[c])
        back_next.append(lax.ppermute(to_prev, AX, backward))
        back_prev.append(lax.ppermute(to_next, AX, forward))
        received += [above[c], below[c]]
    new_density, diagonal = own_products(info, block_mask, work, received, density.shape)
    shares = energy_shares(info, atoms, cell, diagonal)
    gathered = lax.all_to_all(shares, AX, 0, 0, tiled=True)
    energies = charges * jnp.sum(gathered, axis=0).reshape(-1)

    at_next, at_prev = side_products(work)
    partials = []
    for c in chunks:
        partials += [back_next[c], back_prev[c]]
    new_density = finish(info, block_mask, at_next, at_prev, partials, new_density)
    return new_density, energies


def solution(mesh):
    in_specs = (
        P(AX, None, None, None),
        P(AX, None),
        P(AX),
        P(),
        P(None, AX),
        P(AX),
    )
    out_specs = (P(AX, None, None, None), P(AX))
    return jax.shard_map(on_device, mesh=mesh, in_specs=in_specs, out_specs=out_specs, check_vma=False)
```

time: 651 us -> 158 us (0.24)
  waiting for transfers between devices: 258 us -> 0.02 us
  local copies, waits for them, and re-layouts: 145 us -> 5.5 us
  loops' own time: 105 us -> 0 us
  matrix products: 69 us -> 0 us
  Pallas kernels: 0 us -> 62.3 us
  blocking collectives: 0 us -> 54.1 us
  other arithmetic: 43.7 us -> 1.92 us
  starting transfers between devices: 12.2 us -> 32.7 us
  between operations: 14.6 us -> 1.01 us
    reduce_scatter x1 -> x0, waiting for transfers between devices: 123 us -> none  [on_device(): lax.psum_scatter(lax.map(lambda row_id: plane_potential(whole_plane(row_i...]
    another operation x2 -> x0, loops' own time: 105 us -> none  [the longest x1 83.1 us: on_device(): lax.map(lambda row_id: plane_potential(whole_plane(row_id), xcoord, along...]
    ppermute x4 -> x8, waiting for transfers between devices: 78.4 us -> 0.02 us  [the longest x2 0.01 us: on_device(): back_prev.append(lax.ppermute(to_next, AX, forward))]
    dynamic_slice x96 -> x1, local copies, waits for them, and re-layouts: 77.2 us -> 1.24 us  [on_device(): slab_of_device[my_index]]
    dot_general x79 -> x0, matrix products: 69 us -> none  [the longest x32 35.1 us: plane_potential(): jnp.dot(along_y * weight[None, :], along_z.T, precision=lax.Precision.HIG...]
    pallas_call x0 -> x9, Pallas kernels: none -> 62.3 us  [the longest x1 12.5 us: shift_values(): pl.pallas_call(shift_kernel, out_shape=jax.ShapeDtypeStruct(cell.shape, j...]
    all_gather x1 -> x0, waiting for transfers between devices: 56.6 us -> none  [on_device(): lax.all_gather(grid_density.astype(jnp.bfloat16), ('grp', 'row', 'col'),...]
    all_gather x0 -> x3, blocking collectives: none -> 54.1 us  [on_device(): atoms = lax.all_gather(atoms, axis, axis=0, tiled=True)]
  transfers between devices with their start and end apart: 6 -> 9, of which waited for: 4 -> 0; matrix products, arithmetic and copies ran while one was open for 4% -> 0% of each run, Pallas kernels for 0% -> 35%
where the time goes in v1:
time: 158 us
  Pallas kernels  62.3 us (39%)
  blocking collectives  54.1 us (34%)
  starting transfers between devices  32.7 us (21%)
  local copies, waits for them, and re-layouts  5.5 us (3%)
  other arithmetic  1.92 us (1%)
    all_gather x3, blocking collectives, on_device(): atoms = lax.all_gather(atoms, axis, axis=0, tiled=True)  54.1 us
    pallas_call x1, Pallas kernels, shift_values(): pl.pallas_call(shift_kernel, out_shape=jax.ShapeDtypeStruct(cell.shape, j...  12.5 us
    pallas_call x1, Pallas kernels, energy_shares(): pl.pallas_call(energy_kernel, out_shape=jax.ShapeDtypeStruct((members, la...  10.6 us
    pallas_call x2, Pallas kernels, partial_products(): pl.pallas_call(functools.partial(partial_kernel, chunk), out_shape=[jax.S...  9.56 us
    ppermute x2, starting transfers between devices, on_device(): above = [lax.ppermute(packed[2 * c + 1], AX, forward) for c in chunks]  9.56 us
    pallas_call x1, Pallas kernels, own_products(): pl.pallas_call(own_kernel, out_shape=[jax.ShapeDtypeStruct(shape, jnp.bfl...  9.25 us
    ppermute x2, starting transfers between devices, on_device(): back_prev.append(lax.ppermute(to_next, AX, forward))  9.15 us
    all_to_all x1, starting transfers between devices, on_device(): gathered = lax.all_to_all(shares, AX, 0, 0, tiled=True)  8.85 us
  transfers between devices with their start and end apart: 9, of which 0 were waited for; matrix products, arithmetic and copies ran while one was open for 0% of the time, Pallas kernels for 35%

profile of v1, /device:TPU:0, one launch (start us, length us, event | category | flops | bytes accessed | tf_op | source)
XLA Modules:
  0.0 157.5 jit_solution(379378500780544604)
XLA Ops:
  0.6 0.0 copy-start.8
  0.6 0.0 copy-start.9
  0.7 1.2 dynamic_slice.3
  1.9 1.3 pad_add_fusion.info
  3.2 3.6 %pack.1 = (bf16[13,128,128]{2,1,0:T(8,128)(2,1)}, bf16[13,128,128]{2,1,0:T(8,128)(2,1)}, bf16[15,128,128]{2,1,0:T(8,128)(2,1)}, bf16[15,128,128]{2,1,0:T(8,128)(2,1)}) custom-call(s32[3]{0:T(128)} %pad_add_fusion.info, s32[8,15]{1,0:T(8,128)} %mask.7, bf16[8,15,128,128]{3,2,1,0:T(8,128)(2,1)} %density.3), custom_call_target="tpu_custom_call" | custom-call | flops 917504 | bytes 3670016 | tf_op jit(solution)/shard_map/pack/pallas_call | solution.py:94
  6.8 5.0 %collective-permute-start = (bf16[13,128,128]{2,1,0:T(8,128)(2,1)}, bf16[13,128,128]{2,1,0:T(8,128)(2,1)S(1)}, u32[]{:S(2)}, u32[]{:S(2)}) collective-permute-start(bf16[13,128,128]{2,1,0:T(8,128)(2,1)} %get-tuple-element.16), channel_id=1, source_target_pairs={{0,1},{1,2},{2,3},{3,4},{4,5},{5,6},{6,7},{7,8},{8,9},{9,10},{10,1... | collective-permute-start | bytes 1277960 | tf_op jit(solution)/shard_map/ppermute | solution.py:468
  11.8 1.3 collective-permute-start.1
  13.1 4.6 %collective-permute-start.4 = (bf16[15,128,128]{2,1,0:T(8,128)(2,1)}, bf16[15,128,128]{2,1,0:T(8,128)(2,1)S(1)}, u32[]{:S(2)}, u32[]{:S(2)}) collective-permute-start(bf16[15,128,128]{2,1,0:T(8,128)(2,1)} %get-tuple-element.20), channel_id=1, source_target_pairs={{0,1},{1,2},{2,3},{3,4},{4,5},{5,6},{6,7},{7,8},{8,9},{9,10},{10,1... | collective-permute-start | bytes 1474568 | tf_op jit(solution)/shard_map/ppermute | solution.py:468
  17.7 1.3 collective-permute-start.5
  19.0 0.0 copy-done.8
  19.0 0.0 copy-done.9
  19.0 43.3 %all-gather.1 = f32[4,4,512]{2,1,0:T(4,128)S(1)} all-gather(f32[1,4,512]{2,1,0:T(4,128)S(1)} %maximum_bitcast_fusion), channel_id=2, replica_groups=mesh['grp'=4,'row'=2,'col'=4] {'col'}, dimensions={0}, use_global_device_ids=true | all-gather | bytes 40960 | tf_op jit(solution)/shard_map/all_gather | solution.py:473
  62.3 4.6 %all_gather.10 = f32[8,4,512]{2,1,0:T(4,128)S(1)} all-gather(f32[4,4,512]{2,1,0:T(4,128)S(1)} %all-gather.1), channel_id=1, replica_groups=mesh['grp'=4,'row'=2,'col'=4] {'row'}, dimensions={0}, use_global_device_ids=true | all-gather | bytes 98304 | tf_op jit(solution)/shard_map/all_gather | solution.py:473
  66.9 6.2 %all_gather.11.atoms = f32[32,4,512]{2,1,0:T(4,128)} all-gather(f32[8,4,512]{2,1,0:T(4,128)S(1)} %all_gather.10), channel_id=1, replica_groups=mesh['grp'=4,'row'=2,'col'=4] {'grp'}, dimensions={0}, use_global_device_ids=true | all-gather | bytes 327680 | tf_op jit(solution)/shard_map/all_gather | solution.py:473
  73.1 12.5 %shifts.1 = f32[1,1024]{1,0:T(1,128)} custom-call(s32[3]{0:T(128)} %pad_add_fusion.info, f32[32,4,512]{2,1,0:T(4,128)} %all_gather.11.atoms, s32[1,1024]{1,0:T(1,128)} %bitcast.8), custom_call_target="tpu_custom_call" | custom-call | flops 2147483648 | bytes 262144 | tf_op jit(solution)/shard_map/shifts/pallas_call | solution.py:168
  85.6 5.7 %work.1 = bf16[1024,2816]{1,0:T(8,128)(2,1)} custom-call(s32[3]{0:T(128)} %pad_add_fusion.info, s32[8,15]{1,0:T(8,128)} %mask.7, f32[1,1024]{1,0:T(1,128)} %shifts.1, bf16[8,15,128,128]{3,2,1,0:T(8,128)(2,1)} %density.3), custom_call_target="tpu_custom_call" | custom-call | flops 1966080 | bytes 11534336 | tf_op jit(solution)/shard_map/work/pallas_call | solution.py:202
  91.3 0.0 collective-permute-done.above.refs_0_
  91.3 0.0 copy-start.4
  91.3 0.0 collective-permute-done.1.below.refs_1_
  91.3 0.8 copy-done.4
  92.0 0.0 copy-start.5
  92.0 0.8 copy-done.5
  92.8 4.9 %partial0.1 = (bf16[13,128,128]{2,1,0:T(8,128)(2,1)}, bf16[13,128,128]{2,1,0:T(8,128)(2,1)}) custom-call(bf16[1024,2816]{1,0:T(8,128)(2,1)} %work.1, bf16[13,128,128]{2,1,0:T(8,128)(2,1)} %copy-done.4, bf16[13,128,128]{2,1,0:T(8,128)(2,1)} %copy-done.5), custom_call_target="tpu_custom_call" | custom-call | flops 545259520 | bytes 11534336 | tf_op jit(solution)/shard_map/partial0/pallas_call | solution.py:251
  97.7 1.3 collective-permute-start.2
  98.9 4.6 %collective-permute-start.3 = (bf16[13,128,128]{2,1,0:T(8,128)(2,1)}, bf16[13,128,128]{2,1,0:T(8,128)(2,1)S(1)}, u32[]{:S(2)}, u32[]{:S(2)}) collective-permute-start(bf16[13,128,128]{2,1,0:T(8,128)(2,1)} %get-tuple-element.19), channel_id=1, source_target_pairs={{0,1},{1,2},{2,3},{3,4},{4,5},{5,6},{6,7},{7,8},{8,9},{9,10},{10,1... | collective-permute-start | bytes 1277960 | tf_op jit(solution)/shard_map/ppermute | solution.py:482
  103.5 0.0 collective-permute-done.4.above.refs_2_
  103.5 0.0 copy-start
  103.5 0.0 collective-permute-done.5.below.refs_3_
  103.5 0.8 copy-done
  104.3 0.0 copy-start.1
  104.3 0.8 copy-done.1
  105.1 4.7 %partial1.1 = (bf16[15,128,128]{2,1,0:T(8,128)(2,1)}, bf16[15,128,128]{2,1,0:T(8,128)(2,1)}) custom-call(bf16[1024,2816]{1,0:T(8,128)(2,1)} %work.1, bf16[15,128,128]{2,1,0:T(8,128)(2,1)} %copy-done, bf16[15,128,128]{2,1,0:T(8,128)(2,1)} %copy-done.1), custom_call_target="tpu_custom_call" | custom-call | flops 629145600 | bytes 11534336 | tf_op jit(solution)/shard_map/partial1/pallas_call | solution.py:251
  109.8 1.3 collective-permute-start.6
  111.1 4.6 %collective-permute-start.7 = (bf16[15,128,128]{2,1,0:T(8,128)(2,1)}, bf16[15,128,128]{2,1,0:T(8,128)(2,1)S(1)}, u32[]{:S(2)}, u32[]{:S(2)}) collective-permute-start(bf16[15,128,128]{2,1,0:T(8,128)(2,1)} %get-tuple-element.23), channel_id=1, source_target_pairs={{0,1},{1,2},{2,3},{3,4},{4,5},{5,6},{6,7},{7,8},{8,9},{9,10},{10,1... | collective-permute-start | bytes 1474568 | tf_op jit(solution)/shard_map/ppermute | solution.py:482
  115.7 9.3 %own.1 = (bf16[8,15,128,128]{3,2,1,0:T(8,128)(2,1)}, f32[1,1024]{1,0:T(1,128)}) custom-call(s32[3]{0:T(128)} %pad_add_fusion.info, s32[8,15]{1,0:T(8,128)} %mask.7, bf16[1024,2816]{1,0:T(8,128)(2,1)} %work.1, bf16[13,128,128]{2,1,0:T(8,128)(2,1)} %copy-done.4, bf16[13,128,128]{2,1,0:T(8,128)(2,1)} %copy-done.5, bf16[15,128,128]{2,1,0:T(8,128)(2,1)} %copy-done, ...), custom_call_target="tpu_custom_call" | custom-call | flops 4294967296 | bytes 11534336 | tf_op jit(solution)/shard_map/own/pallas_call | solution.py:310
  124.9 10.6 %energy.1 = f32[32,4,128]{2,1,0:T(4,128)} custom-call(s32[3]{0:T(128)} %pad_add_fusion.info, f32[32,4,512]{2,1,0:T(4,128)} %all_gather.11.atoms, s32[1,1024]{1,0:T(1,128)} %bitcast.9, f32[1,1024]{1,0:T(1,128)} %get-tuple-element.25.diagonal), custom_call_target="tpu_custom_call" | custom-call | flops 1610612736 | bytes 262144 | tf_op jit(solution)/shard_map/energy/pallas_call | solution.py:447
  135.6 8.8 %all-to-all-start = ((f32[32,4,128]{2,1,0:T(4,128)}), f32[32,4,128]{2,1,0:T(4,128)S(1)}, u32[]{:S(2)}, u32[]{:S(2)}) async-start(f32[32,4,128]{2,1,0:T(4,128)} %energy.1), calls=%async_computation | async-start | bytes 131072 | tf_op jit(solution)/shard_map/all_to_all | solution.py:486
  144.4 7.1 %side.1 = (f32[28,128,128]{2,1,0:T(8,128)}, f32[28,128,128]{2,1,0:T(8,128)}) custom-call(bf16[1024,2816]{1,0:T(8,128)(2,1)} %work.1), custom_call_target="tpu_custom_call" | custom-call | flops 1056964608 | bytes 11534336 | tf_op jit(solution)/shard_map/side/pallas_call | solution.py:357
  151.6 0.0 all-to-all-done
  151.6 0.6 bitcast_multiply_fusion
  152.2 0.0 collective-permute-done.2.refs_0_
  152.2 0.0 copy-start.6
  152.2 0.0 collective-permute-done.3.refs_1_
  152.2 0.0 copy-start.7
  152.2 0.0 collective-permute-done.6.refs_2_
  152.2 0.0 copy-start.2
  152.2 0.0 collective-permute-done.7.refs_3_
  152.2 0.0 copy-start.3
  152.3 0.7 copy-done.6
  153.0 0.2 copy-done.7
  153.2 0.1 copy-done.2
  153.3 0.2 copy-done.3
  153.4 3.9 %finish.1 = bf16[8,15,128,128]{3,2,1,0:T(8,128)(2,1)} custom-call(s32[3]{0:T(128)} %pad_add_fusion.info, s32[8,15]{1,0:T(8,128)} %mask.7, f32[28,128,128]{2,1,0:T(8,128)} %get-tuple-element.14.at_next, f32[28,128,128]{2,1,0:T(8,128)} %get-tuple-element.15.at_prev, bf16[13,128,128]{2,1,0:T(8,128)(2,1)} %copy-done.6, ...), custom_call_target="tpu_custom_call", output_to_operand_aliasing={{}: (8, {})} | custom-call | flops 2752512 | bytes 7340032 | tf_op jit(solution)/shard_map/finish/pallas_call | solution.py:398
  (2 shorter events, 0.1 us)
Async XLA Ops:
  0.6 18.4 %copy-start.8 = (f32[512]{0:T(512)S(1)}, f32[512]{0:T(512)}, u32[]{:S(2)}) copy-start(f32[512]{0:T(512)} %param.11) | copy-start | bytes 6148
  0.6 18.4 %copy-start.9 = (f32[3,512]{1,0:T(4,128)S(1)}, f32[3,512]{1,0:T(4,128)}, u32[]{:S(2)}) copy-start(f32[3,512]{1,0:T(4,128)} %param.10) | copy-start | bytes 18436
  6.8 84.4 %collective-permute-start = (bf16[13,128,128]{2,1,0:T(8,128)(2,1)}, bf16[13,128,128]{2,1,0:T(8,128)(2,1)S(1)}, u32[]{:S(2)}, u32[]{:S(2)}) collective-permute-start(bf16[13,128,128]{2,1,0:T(8,128)(2,1)} %get-tuple-element.16), channel_id=1, source_target_pairs={{0,1},{1,2},{2,3},{3,4},{4,5},{5,6},{6,7},{7,8},{8,9},{9,10},{10,1... | collective-permute-start | bytes 1277960 | tf_op jit(solution)/shard_map/ppermute | solution.py:468
  11.8 79.5 %collective-permute-start.1 = (bf16[13,128,128]{2,1,0:T(8,128)(2,1)}, bf16[13,128,128]{2,1,0:T(8,128)(2,1)S(1)}, u32[]{:S(2)}, u32[]{:S(2)}) collective-permute-start(bf16[13,128,128]{2,1,0:T(8,128)(2,1)} %get-tuple-element.17), channel_id=1, source_target_pairs={{1,0},{2,1},{3,2},{4,3},{5,4},{6,5},{7,6},{8,7},{9,8},{10,9},{11,1... | collective-permute-start | bytes 1277960 | tf_op jit(solution)/shard_map/ppermute | solution.py:469
  13.1 90.4 %collective-permute-start.4 = (bf16[15,128,128]{2,1,0:T(8,128)(2,1)}, bf16[15,128,128]{2,1,0:T(8,128)(2,1)S(1)}, u32[]{:S(2)}, u32[]{:S(2)}) collective-permute-start(bf16[15,128,128]{2,1,0:T(8,128)(2,1)} %get-tuple-element.20), channel_id=1, source_target_pairs={{0,1},{1,2},{2,3},{3,4},{4,5},{5,6},{6,7},{7,8},{8,9},{9,10},{10,1... | collective-permute-start | bytes 1474568 | tf_op jit(solution)/shard_map/ppermute | solution.py:468
  17.7 85.8 %collective-permute-start.5 = (bf16[15,128,128]{2,1,0:T(8,128)(2,1)}, bf16[15,128,128]{2,1,0:T(8,128)(2,1)S(1)}, u32[]{:S(2)}, u32[]{:S(2)}) collective-permute-start(bf16[15,128,128]{2,1,0:T(8,128)(2,1)} %get-tuple-element.21), channel_id=1, source_target_pairs={{1,0},{2,1},{3,2},{4,3},{5,4},{6,5},{7,6},{8,7},{9,8},{10,9},{11,1... | collective-permute-start | bytes 1474568 | tf_op jit(solution)/shard_map/ppermute | solution.py:469
  91.3 0.8 copy-start.4
  92.0 0.8 copy-start.5
  97.7 54.5 %collective-permute-start.2 = (bf16[13,128,128]{2,1,0:T(8,128)(2,1)}, bf16[13,128,128]{2,1,0:T(8,128)(2,1)S(1)}, u32[]{:S(2)}, u32[]{:S(2)}) collective-permute-start(bf16[13,128,128]{2,1,0:T(8,128)(2,1)} %get-tuple-element.18), channel_id=1, source_target_pairs={{1,0},{2,1},{3,2},{4,3},{5,4},{6,5},{7,6},{8,7},{9,8},{10,9},{11,1... | collective-permute-start | bytes 1277960 | tf_op jit(solution)/shard_map/ppermute | solution.py:481
  98.9 53.3 %collective-permute-start.3 = (bf16[13,128,128]{2,1,0:T(8,128)(2,1)}, bf16[13,128,128]{2,1,0:T(8,128)(2,1)S(1)}, u32[]{:S(2)}, u32[]{:S(2)}) collective-permute-start(bf16[13,128,128]{2,1,0:T(8,128)(2,1)} %get-tuple-element.19), channel_id=1, source_target_pairs={{0,1},{1,2},{2,3},{3,4},{4,5},{5,6},{6,7},{7,8},{8,9},{9,10},{10,1... | collective-permute-start | bytes 1277960 | tf_op jit(solution)/shard_map/ppermute | solution.py:482
  103.5 0.8 copy-start
  104.3 0.8 copy-start.1
  109.8 42.4 %collective-permute-start.6 = (bf16[15,128,128]{2,1,0:T(8,128)(2,1)}, bf16[15,128,128]{2,1,0:T(8,128)(2,1)S(1)}, u32[]{:S(2)}, u32[]{:S(2)}) collective-permute-start(bf16[15,128,128]{2,1,0:T(8,128)(2,1)} %get-tuple-element.22), channel_id=1, source_target_pairs={{1,0},{2,1},{3,2},{4,3},{5,4},{6,5},{7,6},{8,7},{9,8},{10,9},{11,1... | collective-permute-start | bytes 1474568 | tf_op jit(solution)/shard_map/ppermute | solution.py:481
  111.1 41.1 %collective-permute-start.7 = (bf16[15,128,128]{2,1,0:T(8,128)(2,1)}, bf16[15,128,128]{2,1,0:T(8,128)(2,1)S(1)}, u32[]{:S(2)}, u32[]{:S(2)}) collective-permute-start(bf16[15,128,128]{2,1,0:T(8,128)(2,1)} %get-tuple-element.23), channel_id=1, source_target_pairs={{0,1},{1,2},{2,3},{3,4},{4,5},{5,6},{6,7},{7,8},{8,9},{9,10},{10,1... | collective-permute-start | bytes 1474568 | tf_op jit(solution)/shard_map/ppermute | solution.py:482
  135.6 16.0 %all-to-all-start = ((f32[32,4,128]{2,1,0:T(4,128)}), f32[32,4,128]{2,1,0:T(4,128)S(1)}, u32[]{:S(2)}, u32[]{:S(2)}) async-start(f32[32,4,128]{2,1,0:T(4,128)} %energy.1), calls=%async_computation | async-start | bytes 131072 | tf_op jit(solution)/shard_map/all_to_all | solution.py:486
  152.2 0.8 copy-start.6
  152.2 1.0 copy-start.7
  152.2 1.1 copy-start.2
  152.2 1.2 copy-start.3
